TPU v7x, 128 devices: a whole 4x4x4 slice. The times are simulated.
128 devices in a mesh: col: 8 (over x_lo, y), row: 16 (over x_hi, z, core).
Axes of the slice: x: 4 (x_hi: 2, x_lo: 2; x = x_hi * 2 + x_lo), y: 4, z: 4, core: 2. Of those that a mesh axis runs over, the one named last changes fastest.
Arguments:
- sigma_ret: float32 [16384, 16384], P('col', 'row'), may hold values from -0.0625 to 0.0625
- sigma_less: float32 [16384, 16384], P('col', 'row'), may hold values from -0.046875 to 0.046875
- green_less: float32 [16384, 1024], P('row', 'col'), may hold values from -6 to 6
- green_ret: float32 [1024, 16384], P(('col', 'row')), may hold values from -6 to 6
Outputs:
- collision: float32 [16384, 1024], P(('col', 'row'))
All inputs are finite; a program needn't handle non-finite values.
Results may differ from a plain program's by a relative error of at most 0.00007.
Values sent between devices are 32-bit elements; how exact they have to be, the bound alone decides.
A program may use at most 128 MiB of HBM per device.

v0:
```python
import jax
import jax.numpy as jnp
from jax import lax
from jax.sharding import PartitionSpec as P


def both_terms(sigma_ret, sigma_less, lesser_panel, advanced_panel):
    highest = lax.Precision.HIGHEST
    first_term = jnp.dot(
        sigma_ret, lesser_panel, precision=highest, preferred_element_type=jnp.float32
    )
    second_term = jnp.dot(
        sigma_less, advanced_panel, precision=highest, preferred_element_type=jnp.float32
    )
    return first_term + second_term


def on_device(sigma_ret, sigma_less, green_less, green_ret):
    mirrored = lax.all_to_all(green_ret, "row", split_axis=1, concat_axis=0, tiled=True)
    green_adv = jnp.transpose(mirrored)
    lesser_whole, advanced_whole = (
        lax.all_gather(green_less, "col", axis=1, tiled=True),
        lax.all_gather(green_adv, "col", axis=1, tiled=True),
    )
    return lax.psum_scatter(
        both_terms(sigma_ret, sigma_less, lesser_whole, advanced_whole),
        "row",
        scatter_dimension=0,
        tiled=True,
    )


def solution(mesh):
    placed = (P("col", "row"), P("col", "row"), P("row", "col"), P(("col", "row"), None))
    return jax.shard_map(
        on_device, mesh=mesh, in_specs=placed, out_specs=P(("col", "row"), None), check_vma=False
    )
```

profile of v0, /device:TPU:0, one launch (start us, length us, event | category | flops | bytes accessed | tf_op | source)
XLA Modules:
  0.0 269.6 jit_solution(5344826698814561290)
XLA Ops:
  6.5 0.0 all-gather.3.cloned.1.call-start
  6.5 0.7 all-gather.3.cloned.1.call-update
  7.3 0.0 all-gather.5.cloned.1.call-start
  7.3 22.8 %all_to_all.19 = f32[8,16,1024]{2,0,1:T(8,128)} all-to-all(f32[8,16,1024]{2,0,1:T(8,128)} %bitcast.11), channel_id=1, replica_groups=mesh['col'=8,'row'=16] {'row'}, dimensions={1} | all-to-all | bytes 1048576 | tf_op jit(solution)/shard_map/all_to_all | solution.py:19
  30.1 0.0 all-gather.5.cloned.1.call-update
  30.2 0.0 reduce-scatter.2.cloned.1.call-start
  30.2 43.1 %all-gather.3.cloned.1.call-done = f32[1024,1024]{1,0:T(8,128)} async-done(((f32[1024,128]{1,0:T(8,128)}), f32[1024,1024]{1,0:T(8,128)}) %all-gather.3.cloned.1.call-update) | async-done | bytes 4194320 | tf_op jit(solution)/shard_map/all_gather | solution.py:22
  73.3 31.7 %fusion = f32[2048,1024]{1,0:T(8,128)} fusion(f32[2048,1024]{1,0:T(8,128)} %param.4, f32[1024,1024]{1,0:T(8,128)} %all-gather.3.cloned.1.call-done), kind=kOutput, calls=%fused_computation.1 | convolution fusion | flops 25769803776 | bytes 20971520 | tf_op jit(solution)/shard_map/dot_general | solution.py:9
  105.0 24.3 %all-gather.5.cloned.1.call-done = f32[1024,1024]{0,1:T(8,128)} async-done(((f32[1024,128]{0,1:T(8,128)}), f32[1024,1024]{0,1:T(8,128)}) %all-gather.5.cloned.1.call-update) | async-done | bytes 4194320 | tf_op jit(solution)/shard_map/all_gather | solution.py:23
  129.4 32.5 %convolution_add_fusion = f32[2048,1024]{1,0:T(8,128)} fusion(f32[2048,1024]{1,0:T(8,128)} %fusion, f32[2048,1024]{1,0:T(8,128)} %param.5, f32[1024,1024]{0,1:T(8,128)} %all-gather.5.cloned.1.call-done), kind=kOutput, calls=%fused_computation | convolution fusion | flops 25771900928 | bytes 29360128 | tf_op jit(solution)/shard_map/dot_general | solution.py:12
  161.8 0.0 reduce-scatter.2.cloned.1.call-update
  161.9 101.2 %reduce-scatter.2.cloned.1.call-done = f32[128,1024]{1,0:T(8,128)} async-done(((f32[2048,1024]{1,0:T(8,128)}), f32[128,1024]{1,0:T(8,128)}) %reduce-scatter.2.cloned.1.call-update) | async-done | bytes 524304 | tf_op jit(solution)/shard_map/reduce_scatter | solution.py:25
Async XLA Ops:
  6.5 66.8 %all-gather.3.cloned.1.call-start = ((), (), s32[]{:S(2)}) async-start(), calls=%async_computation.2 | async-start | bytes 4718592 | tf_op jit(solution)/shard_map/all_gather | solution.py:22
  7.3 122.1 %all-gather.5.cloned.1.call-start = ((), (), s32[]{:S(2)}) async-start(), calls=%async_computation.3 | async-start | bytes 4718592 | tf_op jit(solution)/shard_map/all_gather | solution.py:23
  30.2 233.0 %reduce-scatter.2.cloned.1.call-start = ((), (), s32[]{:S(2)}) async-start(), calls=%async_computation.4 | async-start | bytes 8912896 | tf_op jit(solution)/shard_map/reduce_scatter | solution.py:25
Sparse Core Ops, SparseCore 0:
  8.9 64.3 all-gather.2
  74.9 54.3 all-gather.4
  162.0 101.0 reduce-scatter.1
where the time goes:
time: 270 us
  waiting for transfers between devices  169 us (63%)
  matrix products  64.2 us (24%)
  blocking collectives  22.8 us (8%)
  between operations  13.1 us (5%)
    reduce_scatter x1, waiting for transfers between devices, on_device(): lax.psum_scatter(both_terms(sigma_ret, sigma_less, lesser_whole, advanced...  101 us
    all_gather x1, waiting for transfers between devices, on_device(): lax.all_gather(green_less, 'col', axis=1, tiled=True)  43.1 us
    dot_general x1, matrix products, both_terms(): jnp.dot(sigma_less, advanced_panel, precision=highest, preferred_element_...  32.5 us
    dot_general x1, matrix products, both_terms(): jnp.dot(sigma_ret, lesser_panel, precision=highest, preferred_element_typ...  31.7 us
    all_gather x1, waiting for transfers between devices, on_device(): lax.all_gather(green_adv, 'col', axis=1, tiled=True)  24.3 us
    all_to_all x1, blocking collectives, on_device(): lax.all_to_all(green_ret, 'row', split_axis=1, concat_axis=0, tiled=True)  22.8 us
  transfers between devices with their start and end apart: 3, of which 3 were waited for; matrix products, arithmetic and copies ran while one was open for 12% of the time, Pallas kernels for 0%

commit v1 on v0

v1 whole, which is shorter than its diff:
```python
import jax
import jax.numpy as jnp
from jax import lax
from jax.experimental import pallas as pl
from jax.experimental.pallas import tpu as pltpu
from jax.sharding import PartitionSpec as P

MESH = pl.DeviceIdType.MESH
F32 = jnp.float32
BF16 = jnp.bfloat16

NY, NZ = 4, 4
COLS, ROWS = 8, 16

DY = (0, 1, 3, 2)
LESSER, ADVANCED = 0, 1
DZ = (2, 1, 3, 0)
TILE = 512
AHEAD = 8


def kernel(
    sigma_ret, sigma_less, green_less, green_ret, out,
    lesser, advanced, mirror, high, low, stage, lesser_w, advanced_w,
    part, part_in, z_in, x_out, x_in, total,
    load_sem, stage_sem, a2a_send, a2a_recv, send, recv,
    chip_send, chip_recv, z_send, z_recv, x_send, x_recv, out_sem,
):
    col, row = lax.axis_index("col"), lax.axis_index("row")
    x_lo, y = col // NY, col % NY
    x_hi, z, core = row // (2 * NZ), (row // 2) % NZ, row % 2

    def at_col(dx, dy):
        return (((x_lo + dx) % 2) * NY + (y + dy) % NY, row)

    def at_row(dx, dz, dcore):
        return (col, ((x_hi + dx) % 2) * 2 * NZ + ((z + dz) % NZ) * 2 + (core + dcore) % 2)

    y_up, y_down, x_pair = at_col(0, 1), at_col(0, NY - 1), at_col(1, 0)

    load_lesser = pltpu.make_async_copy(green_less, lesser.at[0], load_sem.at[0])
    load_mirror = pltpu.make_async_copy(green_ret, mirror, load_sem.at[1])
    load_lesser.start()
    load_mirror.start()

    def stage_copy(matrix, source, t):
        half, p = t // 8, t % 8
        q = p // 2
        dz = jnp.where(q == 0, DZ[0], jnp.where(q == 1, DZ[1], jnp.where(q == 2, DZ[2], DZ[3])))
        block = at_row(p % 2, dz, 1 - half)[1]
        return pltpu.make_async_copy(
            source.at[pl.ds(pl.multiple_of(block * 128, 128), 128), :],
            stage.at[t % AHEAD],
            stage_sem.at[t % AHEAD],
        )

    for t in range(AHEAD):
        stage_copy(0, sigma_ret, t).start()

    barrier = pltpu.get_barrier_semaphore()
    peers = [y_up, y_down, x_pair] + [(col, (row + d) % ROWS) for d in range(1, ROWS)]
    for peer in peers:
        pl.semaphore_signal(barrier, inc=1, device_id=peer, device_id_type=MESH)
    pl.semaphore_wait(barrier, len(peers))

    def remote(src, dst, send_sem, recv_sem, device):
        return pltpu.make_async_remote_copy(
            src_ref=src, dst_ref=dst, send_sem=send_sem, recv_sem=recv_sem,
            device_id=device, device_id_type=MESH,
        )

    load_mirror.wait()
    exchanges = []
    mine = pl.ds(pl.multiple_of(row * 8, 8), 8)
    for d in range(1, ROWS):
        target = (row + d) % ROWS
        exchanges.append(remote(
            mirror.at[:, pl.ds(pl.multiple_of(target * 1024, 1024), 1024)],
            advanced.at[0, mine, :],
            a2a_send.at[d - 1], a2a_recv.at[d - 1], (col, target),
        ))
    own_piece = pltpu.make_async_copy(
        mirror.at[:, pl.ds(pl.multiple_of(row * 1024, 1024), 1024)],
        advanced.at[0, mine, :], load_sem.at[2],
    )
    for copy in exchanges:
        copy.start()
    own_piece.start()

    panels = (lesser, advanced)
    started = []

    def panel_copy(matrix, dst, src, device):
        return remote(
            panels[matrix].at[src], panels[matrix].at[dst],
            send.at[matrix, dst], recv.at[matrix, dst], device,
        )

    def forward(matrix, dst, src, device):
        copy = panel_copy(matrix, dst, src, device)
        copy.start()
        started.append(copy)

    def arrived(matrix, slot):
        panel_copy(matrix, slot, slot, y_up).wait_recv()

    def to_neighbours(matrix):
        forward(matrix, 4, 0, y_up)
        forward(matrix, 2, 0, y_down)
        forward(matrix, 1, 0, x_pair)

    load_lesser.wait()
    to_neighbours(LESSER)

    def split(matrix, source, following):
        def step(t, carry):
            stage_copy(matrix, source, t).wait()
            value = stage[t % AHEAD]
            top = value.astype(BF16)
            rows = pl.ds(pl.multiple_of((t % 8) * 128, 128), 128)
            high[matrix, t // 8, rows, :] = top
            low[matrix, t // 8, rows, :] = (value - top.astype(F32)).astype(BF16)

            @pl.when(t + AHEAD < 16)
            def _():
                stage_copy(matrix, source, t + AHEAD).start()

            if following is not None:
                @pl.when(t + AHEAD >= 16)
                def _():
                    stage_copy(1, following, t + AHEAD - 16).start()
            return carry

        lax.fori_loop(0, 16, step, 0)

    split(0, sigma_ret, sigma_less)
    own_piece.wait()
    for copy in exchanges:
        copy.wait_recv()
    to_neighbours(ADVANCED)
    split(1, sigma_less, None)

    def chip_copy(slot, tile):
        rows = pl.ds(pl.multiple_of(tile * TILE, TILE), TILE)
        return remote(
            part.at[slot, 0, rows, :], part_in.at[slot, rows, :],
            chip_send.at[slot, tile], chip_recv.at[slot, tile], at_row(0, 0, 1),
        )

    def z_copy(slot, p):
        return remote(
            part.at[slot, 1, pl.ds(p * 256, 256), :], z_in.at[slot, p],
            z_send.at[slot, p], z_recv.at[slot, p], at_row(0, DZ[p], 0),
        )

    def x_copy(slot):
        return remote(
            x_out.at[slot], x_in.at[slot], x_send.at[slot], x_recv.at[slot], at_row(1, 0, 0)
        )

    def out_copy(slot):
        owner = at_col(slot % 2, DY[slot // 2])[0]
        return pltpu.make_async_copy(
            total.at[slot],
            out.at[:, pl.ds(pl.multiple_of(owner * 128, 128), 128)],
            out_sem.at[slot],
        )

    def product(slot):
        value = lesser[slot]
        top = value.astype(BF16)
        lesser_w[:, :128] = top
        lesser_w[:, 128:] = (value - top.astype(F32)).astype(BF16)
        value = advanced[slot]
        top = value.astype(BF16)
        advanced_w[:128, :] = top
        advanced_w[128:, :] = (value - top.astype(F32)).astype(BF16)

        def step(t, carry):
            half, tile = t // 2, t % 2
            rows = pl.ds(pl.multiple_of(tile * TILE, TILE), TILE)
            plain, turned = (((1,), (0,)), ((), ())), (((1,), (1,)), ((), ()))
            both = None
            for matrix, weights, dims in ((0, lesser_w, plain), (1, advanced_w, turned)):
                for piece in (high, low):
                    term = lax.dot_general(
                        piece[matrix, half, rows, :], weights[...], dims,
                        preferred_element_type=F32,
                    )
                    both = term if both is None else both + term
            part[slot, half, rows, :] = both[:, :128] + both[:, 128:]

            @pl.when(half == 0)
            def _():
                chip_copy(slot, tile).start()
            return carry

        lax.fori_loop(0, 4, step, 0)

    def chip_sum(slot):
        for tile in range(2):
            rows = pl.ds(tile * TILE, TILE)
            chip_copy(slot, tile).wait_recv()
            part[slot, 1, rows, :] += part_in[slot, rows, :]
            for p in (2 * tile, 2 * tile + 1):
                if p < 3:
                    z_copy(slot, p).start()

    def z_sum(slot):
        for p in range(3):
            z_copy(slot, p).wait_recv()
        own = part[slot, 1, 768:, :]
        summed = (own + z_in[slot, 0]) + (z_in[slot, 1] + z_in[slot, 2])
        total[slot] = summed[:128]
        x_out[slot] = summed[128:]
        x_copy(slot).start()

    def x_sum(slot):
        x_copy(slot).wait_recv()
        total[slot] += x_in[slot]
        out_copy(slot).start()

    for slot in range(8):
        if slot == 1:
            arrived(LESSER, 1)
            forward(LESSER, 5, 1, y_up)
            forward(LESSER, 3, 1, y_down)
            arrived(ADVANCED, 2)
            forward(ADVANCED, 3, 2, x_pair)
            arrived(LESSER, 4)
            forward(LESSER, 6, 4, y_up)
            forward(ADVANCED, 6, 2, y_down)
            arrived(ADVANCED, 4)
            forward(ADVANCED, 5, 4, x_pair)
            arrived(ADVANCED, 1)
        elif slot == 2:
            arrived(LESSER, 2)
        elif slot == 3:
            arrived(LESSER, 5)
            forward(LESSER, 7, 5, y_up)
            arrived(ADVANCED, 3)
            forward(ADVANCED, 7, 3, y_down)
            arrived(LESSER, 3)
        elif slot == 5:
            arrived(ADVANCED, 5)
        elif slot >= 6:
            arrived(LESSER, slot)
            arrived(ADVANCED, slot)
        product(slot)
        chip_sum(slot)
        if slot >= 2:
            z_sum(slot - 2)
        if slot >= 4:
            x_sum(slot - 4)
    for slot in (6, 7):
        z_sum(slot)
        x_sum(slot - 2)
    for slot in (6, 7):
        x_sum(slot)

    for copy in exchanges + started:
        copy.wait_send()
    for slot in range(8):
        for tile in range(2):
            chip_copy(slot, tile).wait_send()
        for p in range(3):
            z_copy(slot, p).wait_send()
        x_copy(slot).wait_send()
        out_copy(slot).wait()


def on_device(sigma_ret, sigma_less, green_less, green_ret):
    dma = pltpu.SemaphoreType.DMA
    return pl.pallas_call(
        kernel,
        out_shape=jax.ShapeDtypeStruct((128, 1024), F32),
        in_specs=[pl.BlockSpec(memory_space=pl.ANY)] * 4,
        out_specs=pl.BlockSpec(memory_space=pl.ANY),
        scratch_shapes=[
            pltpu.VMEM((8, 1024, 128), F32),
            pltpu.VMEM((8, 128, 1024), F32),
            pltpu.VMEM((8, 16384), F32),
            pltpu.VMEM((2, 2, 1024, 1024), BF16),
            pltpu.VMEM((2, 2, 1024, 1024), BF16),
            pltpu.VMEM((AHEAD, 128, 1024), F32),
            pltpu.VMEM((1024, 256), BF16),
            pltpu.VMEM((256, 1024), BF16),
            pltpu.VMEM((8, 2, 1024, 128), F32),
            pltpu.VMEM((8, 1024, 128), F32),
            pltpu.VMEM((8, 3, 256, 128), F32),
            pltpu.VMEM((8, 128, 128), F32),
            pltpu.VMEM((8, 128, 128), F32),
            pltpu.VMEM((8, 128, 128), F32),
            dma((3,)),
            dma((AHEAD,)),
            dma((ROWS - 1,)),
            dma((ROWS - 1,)),
            dma((2, 8)),
            dma((2, 8)),
            dma((8, 2)),
            dma((8, 2)),
            dma((8, 3)),
            dma((8, 3)),
            dma((8,)),
            dma((8,)),
            dma((8,)),
        ],
        compiler_params=pltpu.CompilerParams(
            collective_id=0, has_side_effects=True, vmem_limit_bytes=60 << 20
        ),
        name="collision",
    )(sigma_ret, sigma_less, green_less, green_ret)


def solution(mesh):
    placed = (P("col", "row"), P("col", "row"), P("row", "col"), P(("col", "row"), None))
    return jax.shard_map(
        on_device, mesh=mesh, in_specs=placed, out_specs=P(("col", "row"), None), check_vma=False
    )
```

time: 270 us -> 93.1 us (0.34)
  waiting for transfers between devices: 169 us -> 0 us
  Pallas kernels: 0 us -> 91 us
  matrix products: 64.2 us -> 0 us
  blocking collectives: 22.8 us -> 0 us
  between operations: 13.1 us -> 0.01 us
    reduce_scatter x1 -> x0, waiting for transfers between devices: 101 us -> none  [on_device(): lax.psum_scatter(both_terms(sigma_ret, sigma_less, lesser_whole, advanced...]
    pallas_call x0 -> x1, Pallas kernels: none -> 91 us  [on_device(): pl.pallas_call(kernel, out_shape=jax.ShapeDtypeStruct((128, 1024), F32),...]
    all_gather x2 -> x0, waiting for transfers between devices: 67.4 us -> none  [the longest x1 43.1 us: on_device(): lax.all_gather(green_less, 'col', axis=1, tiled=True)]
    dot_general x2 -> x0, matrix products: 64.2 us -> none  [the longest x1 32.5 us: both_terms(): jnp.dot(sigma_less, advanced_panel, precision=highest, preferred_element_...]
    all_to_all x1 -> x0, blocking collectives: 22.8 us -> none  [on_device(): lax.all_to_all(green_ret, 'row', split_axis=1, concat_axis=0, tiled=True)]
  transfers between devices with their start and end apart: 3 -> 0, of which waited for: 3 -> 0; matrix products, arithmetic and copies ran while one was open for 12% -> 0% of each run, Pallas kernels for 0% -> 0%
where the time goes in v1:
time: 93.1 us; the launch traced here: 92.9 us
  Pallas kernels  91 us (98%)
  local copies, waits for them, and re-layouts  1.89 us (2%)
    pallas_call x1, Pallas kernels, on_device(): pl.pallas_call(kernel, out_shape=jax.ShapeDtypeStruct((128, 1024), F32),...  91 us
    unnamed x1, local copies, waits for them, and re-layouts  1.89 us

profile of v1, /device:TPU:0, one launch (start us, length us, event | category | flops | bytes accessed | tf_op | source)
XLA Modules:
  0.0 92.9 jit_solution(17638027210461407039)
XLA Ops:
  0.0 91.0 %collision.1 = f32[128,1024]{1,0:T(8,128)} custom-call(f32[2048,1024]{1,0:T(8,128)} %sigma_ret.1, f32[2048,1024]{1,0:T(8,128)} %sigma_less.1, f32[1024,128]{1,0:T(8,128)} %green_less.1, f32[8,16384]{1,0:T(8,128)} %green_ret.1), custom_call_target="tpu_custom_call" | custom-call | tf_op jit(solution)/shard_map/collision/pallas_call | solution.py:274
  91.0 1.9 %copy.6 = f32[128,1024]{1,0:T(8,128)} copy(f32[128,1024]{1,0:T(8,128)} %collision.1) | data formatting | bytes 1048576

commit v2 on v1

v2 whole, which is shorter than its diff:
```python
import jax
import jax.numpy as jnp
from jax import lax
from jax.experimental import pallas as pl
from jax.experimental.pallas import tpu as pltpu
from jax.sharding import PartitionSpec as P

MESH = pl.DeviceIdType.MESH
F32 = jnp.float32
BF16 = jnp.bfloat16

NY, NZ = 4, 4
COLS, ROWS = 8, 16

DY = (0, 1, 3, 2)
LESSER, ADVANCED = 0, 1
DZ = (2, 1, 3, 0)
TILE = 512
AHEAD = 8


def kernel(
    sigma_ret, sigma_less, green_less, green_ret, out,
    lesser, advanced, mirror, high, low, stage, lesser_w, advanced_w,
    part, part_in, z_in, x_out, x_in, total,
    load_sem, stage_sem, a2a_send, a2a_recv, send, recv,
    chip_send, chip_recv, z_send, z_recv, x_send, x_recv, far_in, far_send, far_recv, out_sem,
):
    col, row = lax.axis_index("col"), lax.axis_index("row")
    x_lo, y = col // NY, col % NY
    x_hi, z, core = row // (2 * NZ), (row // 2) % NZ, row % 2

    def at_col(dx, dy):
        return (((x_lo + dx) % 2) * NY + (y + dy) % NY, row)

    def at_row(dx, dz, dcore):
        return (col, ((x_hi + dx) % 2) * 2 * NZ + ((z + dz) % NZ) * 2 + (core + dcore) % 2)

    y_up, y_down, x_pair = at_col(0, 1), at_col(0, NY - 1), at_col(1, 0)

    load_lesser = pltpu.make_async_copy(green_less, lesser.at[0], load_sem.at[0])
    load_mirror = pltpu.make_async_copy(green_ret, mirror, load_sem.at[1])
    load_lesser.start()
    load_mirror.start()

    def stage_copy(matrix, source, t):
        half, p = t // 8, t % 8
        q = p // 2
        dz = jnp.where(q == 0, DZ[0], jnp.where(q == 1, DZ[1], jnp.where(q == 2, DZ[2], DZ[3])))
        block = at_row(p % 2, dz, 1 - half)[1]
        return pltpu.make_async_copy(
            source.at[pl.ds(pl.multiple_of(block * 128, 128), 128), :],
            stage.at[t % AHEAD],
            stage_sem.at[t % AHEAD],
        )

    for t in range(AHEAD):
        stage_copy(0, sigma_ret, t).start()

    barrier = pltpu.get_barrier_semaphore()
    peers = [y_up, y_down, x_pair] + [(col, (row + d) % ROWS) for d in range(1, ROWS)]
    for peer in peers:
        pl.semaphore_signal(barrier, inc=1, device_id=peer, device_id_type=MESH)
    pl.semaphore_wait(barrier, len(peers))

    def remote(src, dst, send_sem, recv_sem, device):
        return pltpu.make_async_remote_copy(
            src_ref=src, dst_ref=dst, send_sem=send_sem, recv_sem=recv_sem,
            device_id=device, device_id_type=MESH,
        )

    load_mirror.wait()
    exchanges = []
    mine = pl.ds(pl.multiple_of(row * 8, 8), 8)
    for d in range(1, ROWS):
        target = (row + d) % ROWS
        exchanges.append(remote(
            mirror.at[:, pl.ds(pl.multiple_of(target * 1024, 1024), 1024)],
            advanced.at[0, mine, :],
            a2a_send.at[d - 1], a2a_recv.at[d - 1], (col, target),
        ))
    own_piece = pltpu.make_async_copy(
        mirror.at[:, pl.ds(pl.multiple_of(row * 1024, 1024), 1024)],
        advanced.at[0, mine, :], load_sem.at[2],
    )
    for copy in exchanges:
        copy.start()
    own_piece.start()

    panels = (lesser, advanced)
    started = []

    def panel(matrix, slot, half):
        if half is None:
            return panels[matrix].at[slot]
        times = pl.ds(half * 512, 512)
        return lesser.at[slot, times, :] if matrix == LESSER else advanced.at[slot, :, times]

    def panel_copy(matrix, dst, src, device, half):
        index = (matrix, dst, half or 0)
        return remote(
            panel(matrix, src, half), panel(matrix, dst, half), send.at[index], recv.at[index], device
        )

    def forward(matrix, dst, src, device, half=None):
        copy = panel_copy(matrix, dst, src, device, half)
        copy.start()
        started.append(copy)

    def arrived(matrix, slot, half=None):
        panel_copy(matrix, slot, slot, y_up, half).wait_recv()

    def to_neighbours(matrix):
        forward(matrix, 4, 0, y_up)
        forward(matrix, 2, 0, y_down)
        forward(matrix, 1, 0, x_pair)

    load_lesser.wait()
    to_neighbours(LESSER)

    def split(matrix, source, following):
        def step(t, carry):
            stage_copy(matrix, source, t).wait()
            value = stage[t % AHEAD]
            top = value.astype(BF16)
            rest = (value - top.astype(F32)).astype(BF16)
            for group in range(2):
                rows = pl.ds(pl.multiple_of(group * 512 + (t % 8) * 64, 64), 64)
                high[matrix, t // 8, rows, :] = top[group * 64 : group * 64 + 64]
                low[matrix, t // 8, rows, :] = rest[group * 64 : group * 64 + 64]

            @pl.when(t + AHEAD < 16)
            def _():
                stage_copy(matrix, source, t + AHEAD).start()

            if following is not None:
                @pl.when(t + AHEAD >= 16)
                def _():
                    stage_copy(1, following, t + AHEAD - 16).start()
            return carry

        lax.fori_loop(0, 16, step, 0)

    def chip_copy(slot, tile):
        rows = pl.ds(pl.multiple_of(tile * TILE, TILE), TILE)
        return remote(
            part.at[slot, 0, rows, :], part_in.at[slot, rows, :],
            chip_send.at[slot, tile], chip_recv.at[slot, tile], at_row(0, 0, 1),
        )

    def z_copy(slot, p, group):
        return remote(
            part.at[slot, 1, pl.ds(group * 512 + p * 128, 128), :],
            z_in.at[slot, p, pl.ds(group * 128, 128), :],
            z_send.at[slot, 2 * p + group], z_recv.at[slot, 2 * p + group], at_row(0, DZ[p], 0),
        )

    def x_copy(slot):
        return remote(
            x_out.at[slot], x_in.at[slot], x_send.at[slot], x_recv.at[slot], at_row(1, 0, 0)
        )

    def out_copy(slot):
        owner = at_col(slot % 2, DY[slot // 2])[0]
        return pltpu.make_async_copy(
            total.at[slot],
            out.at[:, pl.ds(pl.multiple_of(owner * 128, 128), 128)],
            out_sem.at[slot],
        )

    def load_weights(slot, parts):
        for matrix, start, count in parts:
            times = pl.ds(start, count)
            if matrix == LESSER:
                value = lesser[slot, times, :]
                top = value.astype(BF16)
                lesser_w[times, :128] = top
                lesser_w[times, 128:] = (value - top.astype(F32)).astype(BF16)
            else:
                value = advanced[slot, :, times]
                top = value.astype(BF16)
                advanced_w[:128, times] = top
                advanced_w[128:, times] = (value - top.astype(F32)).astype(BF16)

    def tile_product(slot, parts, first, half, tile):
        rows = pl.ds(pl.multiple_of(tile * TILE, TILE), TILE)
        both = None
        for matrix, start, count in parts:
            times = pl.ds(start, count)
            if matrix == LESSER:
                weights, dims = lesser_w[times, :], (((1,), (0,)), ((), ()))
            else:
                weights, dims = advanced_w[:, times], (((1,), (1,)), ((), ()))
            for piece in (high, low):
                term = lax.dot_general(
                    piece[matrix, half, rows, times], weights, dims, preferred_element_type=F32
                )
                both = term if both is None else both + term
        both = both[:, :128] + both[:, 128:]
        if first:
            part[slot, half, rows, :] = both
        else:
            part[slot, half, rows, :] += both

    WHOLE = {LESSER: ((LESSER, 0, 1024),), ADVANCED: ((ADVANCED, 0, 1024),)}
    HALVES = [tuple((matrix, start, 512) for matrix in (LESSER, ADVANCED)) for start in (0, 512)]

    def begin(slot, parts):
        load_weights(slot, parts)

        def step(t, carry):
            tile_product(slot, parts, True, t // 2, t % 2)
            return carry

        lax.fori_loop(0, 4, step, 0)

    def finish(slot, parts, first=False):
        load_weights(slot, parts)

        def step(t, carry):
            half, tile = t // 2, t % 2
            tile_product(slot, parts, first, half, tile)

            @pl.when(half == 0)
            def _():
                chip_copy(slot, tile).start()
            return carry

        lax.fori_loop(0, 4, step, 0)
        for tile in range(2):
            chip_sum(slot, tile)
            depart(slot, tile)

    def chip_sum(slot, tile):
        rows = pl.ds(pl.multiple_of(tile * TILE, TILE), TILE)
        chip_copy(slot, tile).wait_recv()
        part[slot, 1, rows, :] += part_in[slot, rows, :]

    def z_total(slot, group):
        for p in range(3):
            z_copy(slot, p, group).wait_recv()
        own = part[slot, 1, group * 512 + 384 : group * 512 + 512, :]
        rows = pl.ds(group * 128, 128)
        return (own + z_in[slot, 0, rows, :]) + (z_in[slot, 1, rows, :] + z_in[slot, 2, rows, :])

    def z_sum(slot):
        for group in range(2):
            summed = z_total(slot, group)
            rows = pl.ds(group * 64, 64)
            total[slot, rows, :] = summed[:64]
            x_out[slot, rows, :] = summed[64:]
        x_copy(slot).start()

    def x_sum(slot):
        x_copy(slot).wait_recv()
        total[slot] += x_in[slot]
        out_copy(slot).start()

    MIXED = (6, 5, 7)

    def mixed_x(slot, p):
        n = MIXED.index(slot)
        return remote(
            part.at[slot, 1, pl.ds(p * 128 + 64, 64), :], far_in.at[n, p],
            far_send.at[n, p], far_recv.at[n, p], at_row(1, 0, 0),
        )

    def mixed_x_then_z(slot, p):
        return remote(
            part.at[slot, 1, pl.ds(p * 128, 64), :], z_in.at[slot, p, :64, :],
            z_send.at[slot, 2 * p], z_recv.at[slot, 2 * p], at_row(0, DZ[p], 0),
        )

    def mixed_z_then_x(slot):
        return remote(
            x_out.at[slot, :64, :], x_in.at[slot, :64, :],
            x_send.at[slot], x_recv.at[slot], at_row(1, 0, 0),
        )

    def depart(slot, group):
        if slot in MIXED and group == 0:
            for p in range(4):
                mixed_x(slot, p).start()
        else:
            for p in range(3):
                z_copy(slot, p, group).start()

    def mixed_sum(slot):
        n = MIXED.index(slot)
        for p in range(4):
            mixed_x(slot, p).wait_recv()
            part[slot, 1, p * 128 : p * 128 + 64, :] += far_in[n, p]
            if p < 3:
                mixed_x_then_z(slot, p).start()
        summed = z_total(slot, 1)
        x_out[slot, :64, :] = summed[64:]
        mixed_z_then_x(slot).start()
        total[slot, 64:, :] = summed[:64]

    def mixed_end(slot):
        mixed_z_then_x(slot).wait_recv()
        total[slot, 64:, :] += x_in[slot, :64, :]
        for p in range(3):
            mixed_x_then_z(slot, p).wait_recv()
        own = part[slot, 1, 384:448, :]
        total[slot, :64, :] = (own + z_in[slot, 0, :64, :]) + (
            z_in[slot, 1, :64, :] + z_in[slot, 2, :64, :]
        )
        out_copy(slot).start()

    def finish_last(slot, parts):
        load_weights(slot, parts)

        def leave(tile, carry):
            tile_product(slot, parts, False, 0, tile)
            chip_copy(slot, tile).start()
            return carry

        def keep(tile, carry):
            tile_product(slot, parts, False, 1, tile)
            chip_sum(slot, tile)
            for group in range(2):
                @pl.when(tile == group)
                def _():
                    depart(slot, group)
            return carry

        lax.fori_loop(0, 2, leave, 0)
        lax.fori_loop(0, 2, keep, 0)

    split(0, sigma_ret, sigma_less)
    begin(0, WHOLE[LESSER])
    split(1, sigma_less, None)
    own_piece.wait()
    for copy in exchanges:
        copy.wait_recv()
    to_neighbours(ADVANCED)
    finish(0, WHOLE[ADVANCED])
    arrived(LESSER, 2)
    begin(2, WHOLE[LESSER])
    arrived(LESSER, 4)
    begin(4, WHOLE[LESSER])
    arrived(LESSER, 1)
    forward(LESSER, 5, 1, y_up)
    forward(LESSER, 3, 1, y_down)
    forward(LESSER, 6, 4, y_up)
    begin(1, WHOLE[LESSER])
    arrived(ADVANCED, 2)
    forward(ADVANCED, 3, 2, x_pair, 0)
    forward(ADVANCED, 3, 2, x_pair, 1)
    forward(ADVANCED, 6, 2, y_down)
    z_sum(0)
    arrived(ADVANCED, 4)
    forward(ADVANCED, 5, 4, x_pair)
    finish(2, WHOLE[ADVANCED])
    finish(4, WHOLE[ADVANCED])
    arrived(ADVANCED, 1)
    finish(1, WHOLE[ADVANCED])
    arrived(LESSER, 5)
    forward(LESSER, 7, 5, y_up, 0)
    forward(LESSER, 7, 5, y_up, 1)
    begin(5, WHOLE[LESSER])
    arrived(ADVANCED, 3, 0)
    forward(ADVANCED, 7, 3, y_down, 0)
    arrived(LESSER, 3)
    begin(3, WHOLE[LESSER])
    z_sum(2)
    arrived(ADVANCED, 3, 1)
    forward(ADVANCED, 7, 3, y_down, 1)
    finish(3, WHOLE[ADVANCED])
    z_sum(4)
    arrived(LESSER, 6)
    arrived(ADVANCED, 6)
    finish(6, WHOLE[LESSER] + WHOLE[ADVANCED], True)
    z_sum(1)
    arrived(LESSER, 7, 0)
    arrived(ADVANCED, 7, 0)
    begin(7, HALVES[0])
    arrived(ADVANCED, 5)
    finish(5, WHOLE[ADVANCED])
    z_sum(3)
    mixed_sum(6)
    arrived(LESSER, 7, 1)
    arrived(ADVANCED, 7, 1)
    finish_last(7, HALVES[1])
    x_sum(0)
    x_sum(2)
    x_sum(4)
    x_sum(1)
    mixed_sum(5)
    x_sum(3)
    mixed_sum(7)
    mixed_end(6)
    mixed_end(5)
    mixed_end(7)

    for copy in exchanges + started:
        copy.wait_send()
    for slot in range(8):
        for tile in range(2):
            chip_copy(slot, tile).wait_send()
        out_copy(slot).wait()
        for p in range(3):
            z_copy(slot, p, 1).wait_send()
        if slot in MIXED:
            for p in range(4):
                mixed_x(slot, p).wait_send()
            for p in range(3):
                mixed_x_then_z(slot, p).wait_send()
            mixed_z_then_x(slot).wait_send()
        else:
            for p in range(3):
                z_copy(slot, p, 0).wait_send()
            x_copy(slot).wait_send()


def on_device(sigma_ret, sigma_less, green_less, green_ret):
    dma = pltpu.SemaphoreType.DMA
    return pl.pallas_call(
        kernel,
        out_shape=jax.ShapeDtypeStruct((128, 1024), F32),
        in_specs=[pl.BlockSpec(memory_space=pltpu.HBM)] * 4,
        out_specs=pl.BlockSpec(memory_space=pl.ANY),
        scratch_shapes=[
            pltpu.VMEM((8, 1024, 128), F32),
            pltpu.VMEM((8, 128, 1024), F32),
            pltpu.VMEM((8, 16384), F32),
            pltpu.VMEM((2, 2, 1024, 1024), BF16),
            pltpu.VMEM((2, 2, 1024, 1024), BF16),
            pltpu.VMEM((AHEAD, 128, 1024), F32),
            pltpu.VMEM((1024, 256), BF16),
            pltpu.VMEM((256, 1024), BF16),
            pltpu.VMEM((8, 2, 1024, 128), F32),
            pltpu.VMEM((8, 1024, 128), F32),
            pltpu.VMEM((8, 3, 256, 128), F32),
            pltpu.VMEM((8, 128, 128), F32),
            pltpu.VMEM((8, 128, 128), F32),
            pltpu.VMEM((8, 128, 128), F32),
            dma((3,)),
            dma((AHEAD,)),
            dma((ROWS - 1,)),
            dma((ROWS - 1,)),
            dma((2, 8, 2)),
            dma((2, 8, 2)),
            dma((8, 2)),
            dma((8, 2)),
            dma((8, 6)),
            dma((8, 6)),
            dma((8,)),
            dma((8,)),
            pltpu.VMEM((3, 4, 64, 128), F32),
            dma((3, 4)),
            dma((3, 4)),
            dma((8,)),
        ],
        compiler_params=pltpu.CompilerParams(
            collective_id=0, has_side_effects=True, vmem_limit_bytes=53 << 20
        ),
        name="collision",
    )(sigma_ret, sigma_less, green_less, green_ret)


def solution(mesh):
    placed = (P("col", "row"), P("col", "row"), P("row", "col"), P(("col", "row"), None))
    return jax.shard_map(
        on_device, mesh=mesh, in_specs=placed, out_specs=P(("col", "row"), None), check_vma=False
    )
```

time: 93.1 us -> 85.2 us (0.915)
  Pallas kernels: 91 us -> 84.3 us
  local copies, waits for them, and re-layouts: 1.89 us -> 0.8 us
    pallas_call x1, Pallas kernels: 91 us -> 84.3 us  [on_device(): pl.pallas_call(kernel, out_shape=jax.ShapeDtypeStruct((128, 1024), F32),...]
    unnamed x1, local copies, waits for them, and re-layouts: 1.89 us -> 0.8 us
where the time goes in v2:
time: 85.2 us; the launch traced here: 85.1 us
  Pallas kernels  84.3 us (99%)
    pallas_call x1, Pallas kernels, on_device(): pl.pallas_call(kernel, out_shape=jax.ShapeDtypeStruct((128, 1024), F32),...  84.3 us

profile of v2, /device:TPU:0, one launch (start us, length us, event | category | flops | bytes accessed | tf_op | source)
XLA Modules:
  0.0 85.1 jit_solution(9838498493022990486)
XLA Ops:
  0.0 84.3 %collision.1 = f32[128,1024]{1,0:T(8,128)S(1)} custom-call(f32[2048,1024]{1,0:T(8,128)} %sigma_ret.1, f32[2048,1024]{1,0:T(8,128)} %sigma_less.1, f32[1024,128]{1,0:T(8,128)} %green_less.1, f32[8,16384]{1,0:T(8,128)} %green_ret.1), custom_call_target="tpu_custom_call" | custom-call | tf_op jit(solution)/shard_map/collision/pallas_call | solution.py:419
  84.3 0.8 copy.6

commit v3 on v2

--- a/solution.py
+++ b/solution.py
@@ -24,7 +24,7 @@
     lesser, advanced, mirror, high, low, stage, lesser_w, advanced_w,
     part, part_in, z_in, x_out, x_in, total,
     load_sem, stage_sem, a2a_send, a2a_recv, send, recv,
-    chip_send, chip_recv, z_send, z_recv, x_send, x_recv, far_in, far_send, far_recv, out_sem,
+    chip_send, chip_recv, z_send, z_recv, x_send, x_recv, far_in, far_send, far_recv, out_sem, ready_sem,
 ):
     col, row = lax.axis_index("col"), lax.axis_index("row")
     x_lo, y = col // NY, col % NY
@@ -57,17 +57,53 @@
     for t in range(AHEAD):
         stage_copy(0, sigma_ret, t).start()
 
-    barrier = pltpu.get_barrier_semaphore()
-    peers = [y_up, y_down, x_pair] + [(col, (row + d) % ROWS) for d in range(1, ROWS)]
-    for peer in peers:
-        pl.semaphore_signal(barrier, inc=1, device_id=peer, device_id_type=MESH)
-    pl.semaphore_wait(barrier, len(peers))
+    def meet(semaphore, peers):
+        for peer in peers:
+            pl.semaphore_signal(semaphore, inc=1, device_id=peer, device_id_type=MESH)
+        pl.semaphore_wait(semaphore, len(peers))
+
+    z_mates = [at_row(0, d, 0) for d in range(1, NZ)]
+    chip_mate = at_row(0, 0, 1)
+    meet(
+        pltpu.get_barrier_semaphore(),
+        [y_up, y_down, x_pair, chip_mate, at_row(1, 0, 0)] + z_mates,
+    )
 
     def remote(src, dst, send_sem, recv_sem, device):
         return pltpu.make_async_remote_copy(
             src_ref=src, dst_ref=dst, send_sem=send_sem, recv_sem=recv_sem,
             device_id=device, device_id_type=MESH,
         )
+
+    panels = (lesser, advanced)
+    started = []
+
+    def panel(matrix, slot, half):
+        if half is None:
+            return panels[matrix].at[slot]
+        times = pl.ds(half * 512, 512)
+        return lesser.at[slot, times, :] if matrix == LESSER else advanced.at[slot, :, times]
+
+    def panel_copy(matrix, dst, src, device, half):
+        index = (matrix, dst, half or 0)
+        return remote(
+            panel(matrix, src, half), panel(matrix, dst, half), send.at[index], recv.at[index], device
+        )
+
+    def forward(matrix, dst, src, device, half=None):
+        copy = panel_copy(matrix, dst, src, device, half)
+        copy.start()
+        started.append(copy)
+
+    def arrived(matrix, slot, half=None):
+        panel_copy(matrix, slot, slot, y_up, half).wait_recv()
+
+    load_lesser.wait()
+    forward(LESSER, 4, 0, y_up)
+    forward(LESSER, 2, 0, y_down)
+
+    meet(ready_sem.at[0], z_mates)
+    meet(ready_sem.at[1], [chip_mate])
 
     load_mirror.wait()
     exchanges = []
@@ -86,37 +122,8 @@
     for copy in exchanges:
         copy.start()
     own_piece.start()
-
-    panels = (lesser, advanced)
-    started = []
-
-    def panel(matrix, slot, half):
-        if half is None:
-            return panels[matrix].at[slot]
-        times = pl.ds(half * 512, 512)
-        return lesser.at[slot, times, :] if matrix == LESSER else advanced.at[slot, :, times]
-
-    def panel_copy(matrix, dst, src, device, half):
-        index = (matrix, dst, half or 0)
-        return remote(
-            panel(matrix, src, half), panel(matrix, dst, half), send.at[index], recv.at[index], device
-        )
-
-    def forward(matrix, dst, src, device, half=None):
-        copy = panel_copy(matrix, dst, src, device, half)
-        copy.start()
-        started.append(copy)
-
-    def arrived(matrix, slot, half=None):
-        panel_copy(matrix, slot, slot, y_up, half).wait_recv()
-
-    def to_neighbours(matrix):
-        forward(matrix, 4, 0, y_up)
-        forward(matrix, 2, 0, y_down)
-        forward(matrix, 1, 0, x_pair)
-
-    load_lesser.wait()
-    to_neighbours(LESSER)
+    forward(LESSER, 1, 0, x_pair)
+
 
     def split(matrix, source, following):
         def step(t, carry):
@@ -182,8 +189,8 @@
                 advanced_w[:128, times] = top
                 advanced_w[128:, times] = (value - top.astype(F32)).astype(BF16)
 
-    def tile_product(slot, parts, first, half, tile):
-        rows = pl.ds(pl.multiple_of(tile * TILE, TILE), TILE)
+    def tile_product(slot, parts, first, half, tile, height=TILE):
+        rows = pl.ds(pl.multiple_of(tile * height, height), height)
         both = None
         for matrix, start, count in parts:
             times = pl.ds(start, count)
@@ -208,25 +215,22 @@
     def begin(slot, parts):
         load_weights(slot, parts)
 
-        def step(t, carry):
-            tile_product(slot, parts, True, t // 2, t % 2)
+        def step(half, carry):
+            tile_product(slot, parts, True, half, 0, 2 * TILE)
             return carry
 
-        lax.fori_loop(0, 4, step, 0)
-
-    def finish(slot, parts, first=False):
+        lax.fori_loop(0, 2, step, 0)
+
+    def finish(slot, parts):
         load_weights(slot, parts)
 
-        def step(t, carry):
-            half, tile = t // 2, t % 2
-            tile_product(slot, parts, first, half, tile)
-
-            @pl.when(half == 0)
-            def _():
-                chip_copy(slot, tile).start()
+        def step(tile, carry):
+            tile_product(slot, parts, False, 0, tile)
+            chip_copy(slot, tile).start()
             return carry
 
-        lax.fori_loop(0, 4, step, 0)
+        lax.fori_loop(0, 2, step, 0)
+        tile_product(slot, parts, False, 1, 0, 2 * TILE)
         for tile in range(2):
             chip_sum(slot, tile)
             depart(slot, tile)
@@ -256,7 +260,7 @@
         total[slot] += x_in[slot]
         out_copy(slot).start()
 
-    MIXED = (6, 5, 7)
+    MIXED = (5, 7)
 
     def mixed_x(slot, p):
         n = MIXED.index(slot)
@@ -334,7 +338,9 @@
     own_piece.wait()
     for copy in exchanges:
         copy.wait_recv()
-    to_neighbours(ADVANCED)
+    forward(ADVANCED, 4, 0, y_up)
+    forward(ADVANCED, 2, 0, y_down)
+    forward(ADVANCED, 1, 0, x_pair)
     finish(0, WHOLE[ADVANCED])
     arrived(LESSER, 2)
     begin(2, WHOLE[LESSER])
@@ -343,12 +349,14 @@
     arrived(LESSER, 1)
     forward(LESSER, 5, 1, y_up)
     forward(LESSER, 3, 1, y_down)
-    forward(LESSER, 6, 4, y_up)
+    forward(LESSER, 6, 4, y_up, 0)
+    forward(LESSER, 6, 4, y_up, 1)
     begin(1, WHOLE[LESSER])
     arrived(ADVANCED, 2)
     forward(ADVANCED, 3, 2, x_pair, 0)
     forward(ADVANCED, 3, 2, x_pair, 1)
-    forward(ADVANCED, 6, 2, y_down)
+    forward(ADVANCED, 6, 2, y_down, 0)
+    forward(ADVANCED, 6, 2, y_down, 1)
     z_sum(0)
     arrived(ADVANCED, 4)
     forward(ADVANCED, 5, 4, x_pair)
@@ -369,20 +377,23 @@
     forward(ADVANCED, 7, 3, y_down, 1)
     finish(3, WHOLE[ADVANCED])
     z_sum(4)
-    arrived(LESSER, 6)
-    arrived(ADVANCED, 6)
-    finish(6, WHOLE[LESSER] + WHOLE[ADVANCED], True)
+    arrived(LESSER, 6, 0)
+    arrived(ADVANCED, 6, 0)
+    begin(6, HALVES[0])
     z_sum(1)
+    arrived(LESSER, 6, 1)
+    arrived(ADVANCED, 6, 1)
+    finish(6, HALVES[1])
     arrived(LESSER, 7, 0)
     arrived(ADVANCED, 7, 0)
     begin(7, HALVES[0])
     arrived(ADVANCED, 5)
     finish(5, WHOLE[ADVANCED])
     z_sum(3)
-    mixed_sum(6)
     arrived(LESSER, 7, 1)
     arrived(ADVANCED, 7, 1)
     finish_last(7, HALVES[1])
+    z_sum(6)
     x_sum(0)
     x_sum(2)
     x_sum(4)
@@ -390,7 +401,7 @@
     mixed_sum(5)
     x_sum(3)
     mixed_sum(7)
-    mixed_end(6)
+    x_sum(6)
     mixed_end(5)
     mixed_end(7)
 
@@ -448,10 +459,11 @@
             dma((8, 6)),
             dma((8,)),
             dma((8,)),
-            pltpu.VMEM((3, 4, 64, 128), F32),
-            dma((3, 4)),
-            dma((3, 4)),
+            pltpu.VMEM((2, 4, 64, 128), F32),
+            dma((2, 4)),
+            dma((2, 4)),
             dma((8,)),
+            pltpu.SemaphoreType.REGULAR((2,)),
         ],
         compiler_params=pltpu.CompilerParams(
             collective_id=0, has_side_effects=True, vmem_limit_bytes=53 << 20

time: 85.2 us -> 83.1 us (0.975)
  Pallas kernels: 84.3 us -> 82.1 us
    pallas_call x1, Pallas kernels: 84.3 us -> 82.1 us  [on_device(): pl.pallas_call(kernel, out_shape=jax.ShapeDtypeStruct((128, 1024), F32),...]
where the time goes in v3:
time: 83.1 us; the launch traced here: 82.9 us
  Pallas kernels  82.1 us (99%)
    pallas_call x1, Pallas kernels, on_device(): pl.pallas_call(kernel, out_shape=jax.ShapeDtypeStruct((128, 1024), F32),...  82.1 us

profile of v3, /device:TPU:0, one launch (start us, length us, event | category | flops | bytes accessed | tf_op | source)
XLA Modules:
  0.0 82.9 jit_solution(1472420345067498278)
XLA Ops:
  0.0 82.1 %collision.1 = f32[128,1024]{1,0:T(8,128)S(1)} custom-call(f32[2048,1024]{1,0:T(8,128)} %sigma_ret.1, f32[2048,1024]{1,0:T(8,128)} %sigma_less.1, f32[1024,128]{1,0:T(8,128)} %green_less.1, f32[8,16384]{1,0:T(8,128)} %green_ret.1), custom_call_target="tpu_custom_call" | custom-call | tf_op jit(solution)/shard_map/collision/pallas_call | solution.py:430
  82.1 0.8 copy.6

commit v4 on v3

--- a/solution.py
+++ b/solution.py
@@ -76,7 +76,6 @@
         )
 
     panels = (lesser, advanced)
-    started = []
 
     def panel(matrix, slot, half):
         if half is None:
@@ -87,13 +86,12 @@
     def panel_copy(matrix, dst, src, device, half):
         index = (matrix, dst, half or 0)
         return remote(
-            panel(matrix, src, half), panel(matrix, dst, half), send.at[index], recv.at[index], device
+            panel(matrix, src, half), panel(matrix, dst, half), send, recv.at[index], device
         )
 
     def forward(matrix, dst, src, device, half=None):
         copy = panel_copy(matrix, dst, src, device, half)
         copy.start()
-        started.append(copy)
 
     def arrived(matrix, slot, half=None):
         panel_copy(matrix, slot, slot, y_up, half).wait_recv()
@@ -104,6 +102,9 @@
 
     meet(ready_sem.at[0], z_mates)
     meet(ready_sem.at[1], [chip_mate])
+
+    def wait_bytes(semaphore, ref):
+        pltpu.make_async_copy(ref, ref, semaphore).wait()
 
     load_mirror.wait()
     exchanges = []
@@ -113,7 +114,7 @@
         exchanges.append(remote(
             mirror.at[:, pl.ds(pl.multiple_of(target * 1024, 1024), 1024)],
             advanced.at[0, mine, :],
-            a2a_send.at[d - 1], a2a_recv.at[d - 1], (col, target),
+            a2a_send, a2a_recv, (col, target),
         ))
     own_piece = pltpu.make_async_copy(
         mirror.at[:, pl.ds(pl.multiple_of(row * 1024, 1024), 1024)],
@@ -148,23 +149,26 @@
 
         lax.fori_loop(0, 16, step, 0)
 
+    MIXED = (5, 7)
+
     def chip_copy(slot, tile):
         rows = pl.ds(pl.multiple_of(tile * TILE, TILE), TILE)
         return remote(
             part.at[slot, 0, rows, :], part_in.at[slot, rows, :],
-            chip_send.at[slot, tile], chip_recv.at[slot, tile], at_row(0, 0, 1),
+            chip_send, chip_recv.at[slot, tile], at_row(0, 0, 1),
         )
 
     def z_copy(slot, p, group):
         return remote(
             part.at[slot, 1, pl.ds(group * 512 + p * 128, 128), :],
             z_in.at[slot, p, pl.ds(group * 128, 128), :],
-            z_send.at[slot, 2 * p + group], z_recv.at[slot, 2 * p + group], at_row(0, DZ[p], 0),
+            z_send.at[MIXED.index(slot) + 1 if slot in MIXED else 0], z_recv.at[slot, group],
+            at_row(0, DZ[p], 0),
         )
 
     def x_copy(slot):
         return remote(
-            x_out.at[slot], x_in.at[slot], x_send.at[slot], x_recv.at[slot], at_row(1, 0, 0)
+            x_out.at[slot], x_in.at[slot], x_send.at[0], x_recv.at[slot], at_row(1, 0, 0)
         )
 
     def out_copy(slot):
@@ -172,7 +176,7 @@
         return pltpu.make_async_copy(
             total.at[slot],
             out.at[:, pl.ds(pl.multiple_of(owner * 128, 128), 128)],
-            out_sem.at[slot],
+            out_sem,
         )
 
     def load_weights(slot, parts):
@@ -212,11 +216,11 @@
     WHOLE = {LESSER: ((LESSER, 0, 1024),), ADVANCED: ((ADVANCED, 0, 1024),)}
     HALVES = [tuple((matrix, start, 512) for matrix in (LESSER, ADVANCED)) for start in (0, 512)]
 
-    def begin(slot, parts):
+    def begin(slot, parts, first=True):
         load_weights(slot, parts)
 
         def step(half, carry):
-            tile_product(slot, parts, True, half, 0, 2 * TILE)
+            tile_product(slot, parts, first, half, 0, 2 * TILE)
             return carry
 
         lax.fori_loop(0, 2, step, 0)
@@ -241,8 +245,7 @@
         part[slot, 1, rows, :] += part_in[slot, rows, :]
 
     def z_total(slot, group):
-        for p in range(3):
-            z_copy(slot, p, group).wait_recv()
+        wait_bytes(z_recv.at[slot, group], z_in.at[slot, :, pl.ds(group * 128, 128), :])
         own = part[slot, 1, group * 512 + 384 : group * 512 + 512, :]
         rows = pl.ds(group * 128, 128)
         return (own + z_in[slot, 0, rows, :]) + (z_in[slot, 1, rows, :] + z_in[slot, 2, rows, :])
@@ -260,25 +263,24 @@
         total[slot] += x_in[slot]
         out_copy(slot).start()
 
-    MIXED = (5, 7)
 
     def mixed_x(slot, p):
         n = MIXED.index(slot)
         return remote(
             part.at[slot, 1, pl.ds(p * 128 + 64, 64), :], far_in.at[n, p],
-            far_send.at[n, p], far_recv.at[n, p], at_row(1, 0, 0),
+            far_send, far_recv.at[n, p], at_row(1, 0, 0),
         )
 
     def mixed_x_then_z(slot, p):
         return remote(
             part.at[slot, 1, pl.ds(p * 128, 64), :], z_in.at[slot, p, :64, :],
-            z_send.at[slot, 2 * p], z_recv.at[slot, 2 * p], at_row(0, DZ[p], 0),
+            z_send.at[MIXED.index(slot) + 1], z_recv.at[slot, 0], at_row(0, DZ[p], 0),
         )
 
     def mixed_z_then_x(slot):
         return remote(
             x_out.at[slot, :64, :], x_in.at[slot, :64, :],
-            x_send.at[slot], x_recv.at[slot], at_row(1, 0, 0),
+            x_send.at[1], x_recv.at[slot], at_row(1, 0, 0),
         )
 
     def depart(slot, group):
@@ -304,8 +306,7 @@
     def mixed_end(slot):
         mixed_z_then_x(slot).wait_recv()
         total[slot, 64:, :] += x_in[slot, :64, :]
-        for p in range(3):
-            mixed_x_then_z(slot, p).wait_recv()
+        wait_bytes(z_recv.at[slot, 0], z_in.at[slot, :, pl.ds(0, 64), :])
         own = part[slot, 1, 384:448, :]
         total[slot, :64, :] = (own + z_in[slot, 0, :64, :]) + (
             z_in[slot, 1, :64, :] + z_in[slot, 2, :64, :]
@@ -336,8 +337,7 @@
     begin(0, WHOLE[LESSER])
     split(1, sigma_less, None)
     own_piece.wait()
-    for copy in exchanges:
-        copy.wait_recv()
+    wait_bytes(a2a_recv, advanced.at[0, pl.ds(0, 120), :])
     forward(ADVANCED, 4, 0, y_up)
     forward(ADVANCED, 2, 0, y_down)
     forward(ADVANCED, 1, 0, x_pair)
@@ -359,7 +359,8 @@
     forward(ADVANCED, 6, 2, y_down, 1)
     z_sum(0)
     arrived(ADVANCED, 4)
-    forward(ADVANCED, 5, 4, x_pair)
+    forward(ADVANCED, 5, 4, x_pair, 0)
+    forward(ADVANCED, 5, 4, x_pair, 1)
     finish(2, WHOLE[ADVANCED])
     finish(4, WHOLE[ADVANCED])
     arrived(ADVANCED, 1)
@@ -371,58 +372,50 @@
     arrived(ADVANCED, 3, 0)
     forward(ADVANCED, 7, 3, y_down, 0)
     arrived(LESSER, 3)
-    begin(3, WHOLE[LESSER])
+    begin(3, WHOLE[LESSER] + ((ADVANCED, 0, 512),))
     z_sum(2)
     arrived(ADVANCED, 3, 1)
     forward(ADVANCED, 7, 3, y_down, 1)
-    finish(3, WHOLE[ADVANCED])
-    z_sum(4)
+    finish(3, ((ADVANCED, 512, 512),))
     arrived(LESSER, 6, 0)
     arrived(ADVANCED, 6, 0)
     begin(6, HALVES[0])
-    z_sum(1)
     arrived(LESSER, 6, 1)
     arrived(ADVANCED, 6, 1)
     finish(6, HALVES[1])
+    arrived(ADVANCED, 5, 0)
+    begin(5, ((ADVANCED, 0, 512),), False)
+    for slot in (4, 1):
+        z_sum(slot)
     arrived(LESSER, 7, 0)
     arrived(ADVANCED, 7, 0)
     begin(7, HALVES[0])
-    arrived(ADVANCED, 5)
-    finish(5, WHOLE[ADVANCED])
     z_sum(3)
+    arrived(ADVANCED, 5, 1)
+    finish(5, ((ADVANCED, 512, 512),))
     arrived(LESSER, 7, 1)
     arrived(ADVANCED, 7, 1)
     finish_last(7, HALVES[1])
     z_sum(6)
-    x_sum(0)
-    x_sum(2)
-    x_sum(4)
-    x_sum(1)
     mixed_sum(5)
+    for slot in (0, 2, 4, 1):
+        x_sum(slot)
+    mixed_sum(7)
     x_sum(3)
-    mixed_sum(7)
     x_sum(6)
     mixed_end(5)
     mixed_end(7)
 
-    for copy in exchanges + started:
-        copy.wait_send()
-    for slot in range(8):
-        for tile in range(2):
-            chip_copy(slot, tile).wait_send()
-        out_copy(slot).wait()
-        for p in range(3):
-            z_copy(slot, p, 1).wait_send()
-        if slot in MIXED:
-            for p in range(4):
-                mixed_x(slot, p).wait_send()
-            for p in range(3):
-                mixed_x_then_z(slot, p).wait_send()
-            mixed_z_then_x(slot).wait_send()
-        else:
-            for p in range(3):
-                z_copy(slot, p, 0).wait_send()
-            x_copy(slot).wait_send()
+    wait_bytes(out_sem, total)
+    wait_bytes(a2a_send, mirror.at[:, pl.ds(0, 15 * 1024)])
+    wait_bytes(send, part.at[pl.ds(0, 7)])
+    wait_bytes(chip_send, part_in)
+    wait_bytes(z_send.at[0], z_in.at[pl.ds(0, 6)])
+    for n in range(2):
+        wait_bytes(z_send.at[n + 1], z_in.at[MIXED[n], :, pl.ds(0, 192), :])
+    wait_bytes(x_send.at[0], x_out.at[pl.ds(0, 6)])
+    wait_bytes(x_send.at[1], x_out.at[6])
+    wait_bytes(far_send, far_in)
 
 
 def on_device(sigma_ret, sigma_less, green_less, green_ret):
@@ -449,20 +442,20 @@
             pltpu.VMEM((8, 128, 128), F32),
             dma((3,)),
             dma((AHEAD,)),
-            dma((ROWS - 1,)),
-            dma((ROWS - 1,)),
+            dma(()),
+            dma(()),
+            dma(()),
             dma((2, 8, 2)),
-            dma((2, 8, 2)),
+            dma(()),
             dma((8, 2)),
+            dma((3,)),
             dma((8, 2)),
-            dma((8, 6)),
-            dma((8, 6)),
-            dma((8,)),
+            dma((2,)),
             dma((8,)),
             pltpu.VMEM((2, 4, 64, 128), F32),
+            dma(()),
             dma((2, 4)),
-            dma((2, 4)),
-            dma((8,)),
+            dma(()),
             pltpu.SemaphoreType.REGULAR((2,)),
         ],
         compiler_params=pltpu.CompilerParams(

time: 83.1 us -> 81.3 us (0.978)
  Pallas kernels: 82.1 us -> 80.4 us
    pallas_call x1, Pallas kernels: 82.1 us -> 80.4 us  [on_device(): pl.pallas_call(kernel, out_shape=jax.ShapeDtypeStruct((128, 1024), F32),...]
where the time goes in v4:
time: 81.3 us; the launch traced here: 81.2 us
  Pallas kernels  80.4 us (99%)
    pallas_call x1, Pallas kernels, on_device(): pl.pallas_call(kernel, out_shape=jax.ShapeDtypeStruct((128, 1024), F32),...  80.4 us

profile of v4, /device:TPU:0, one launch (start us, length us, event | category | flops | bytes accessed | tf_op | source)
XLA Modules:
  0.0 81.2 jit_solution(10199665022995275175)
XLA Ops:
  0.0 80.4 %collision.1 = f32[128,1024]{1,0:T(8,128)S(1)} custom-call(f32[2048,1024]{1,0:T(8,128)} %sigma_ret.1, f32[2048,1024]{1,0:T(8,128)} %sigma_less.1, f32[1024,128]{1,0:T(8,128)} %green_less.1, f32[8,16384]{1,0:T(8,128)} %green_ret.1), custom_call_target="tpu_custom_call" | custom-call | tf_op jit(solution)/shard_map/collision/pallas_call | solution.py:423
  80.4 0.8 copy.6

commit v5 on v4

--- a/solution.py
+++ b/solution.py
@@ -10,7 +10,6 @@
 BF16 = jnp.bfloat16
 
 NY, NZ = 4, 4
-COLS, ROWS = 8, 16
 
 DY = (0, 1, 3, 2)
 LESSER, ADVANCED = 0, 1
@@ -57,17 +56,18 @@
     for t in range(AHEAD):
         stage_copy(0, sigma_ret, t).start()
 
-    def meet(semaphore, peers):
+    def tell(semaphore, peers):
         for peer in peers:
             pl.semaphore_signal(semaphore, inc=1, device_id=peer, device_id_type=MESH)
-        pl.semaphore_wait(semaphore, len(peers))
 
     z_mates = [at_row(0, d, 0) for d in range(1, NZ)]
-    chip_mate = at_row(0, 0, 1)
-    meet(
-        pltpu.get_barrier_semaphore(),
-        [y_up, y_down, x_pair, chip_mate, at_row(1, 0, 0)] + z_mates,
-    )
+    near_row = [(1, 0, 0), (1, 0, 1)] + [(0, d, c) for d in (2, 1, 3) for c in (0, 1)] + [(0, 0, 1)]
+    far_row = [(1, d, c) for d in (2, 1, 3) for c in (0, 1)]
+    near = [y_up, y_down, x_pair] + [at_row(*place) for place in near_row]
+    barrier = pltpu.get_barrier_semaphore()
+    tell(barrier, near)
+    pl.semaphore_wait(barrier, len(near))
+    tell(ready_sem, z_mates)
 
     def remote(src, dst, send_sem, recv_sem, device):
         return pltpu.make_async_remote_copy(
@@ -100,31 +100,29 @@
     forward(LESSER, 4, 0, y_up)
     forward(LESSER, 2, 0, y_down)
 
-    meet(ready_sem.at[0], z_mates)
-    meet(ready_sem.at[1], [chip_mate])
-
     def wait_bytes(semaphore, ref):
         pltpu.make_async_copy(ref, ref, semaphore).wait()
 
+    mine = pl.ds(pl.multiple_of(row * 8, 8), 8)
+
+    def columns_of(target):
+        return mirror.at[:, pl.ds(pl.multiple_of(target * 1024, 1024), 1024)]
+
+    def exchange(place):
+        target = at_row(*place)
+        remote(
+            columns_of(target[1]), advanced.at[0, mine, :], a2a_send, a2a_recv, target
+        ).start()
+
     load_mirror.wait()
-    exchanges = []
-    mine = pl.ds(pl.multiple_of(row * 8, 8), 8)
-    for d in range(1, ROWS):
-        target = (row + d) % ROWS
-        exchanges.append(remote(
-            mirror.at[:, pl.ds(pl.multiple_of(target * 1024, 1024), 1024)],
-            advanced.at[0, mine, :],
-            a2a_send, a2a_recv, (col, target),
-        ))
-    own_piece = pltpu.make_async_copy(
-        mirror.at[:, pl.ds(pl.multiple_of(row * 1024, 1024), 1024)],
-        advanced.at[0, mine, :], load_sem.at[2],
-    )
-    for copy in exchanges:
-        copy.start()
+    for place in near_row:
+        exchange(place)
+    own_piece = pltpu.make_async_copy(columns_of(row), advanced.at[0, mine, :], load_sem.at[2])
     own_piece.start()
+    pl.semaphore_wait(ready_sem, len(z_mates))
+    for place in far_row:
+        exchange(place)
     forward(LESSER, 1, 0, x_pair)
-
 
     def split(matrix, source, following):
         def step(t, carry):
@@ -456,7 +454,7 @@
             dma(()),
             dma((2, 4)),
             dma(()),
-            pltpu.SemaphoreType.REGULAR((2,)),
+            pltpu.SemaphoreType.REGULAR,
         ],
         compiler_params=pltpu.CompilerParams(
             collective_id=0, has_side_effects=True, vmem_limit_bytes=53 << 20

time: 81.3 us -> 80.3 us (0.988)
  Pallas kernels: 80.4 us -> 79.4 us
    pallas_call x1, Pallas kernels: 80.4 us -> 79.4 us  [on_device(): pl.pallas_call(kernel, out_shape=jax.ShapeDtypeStruct((128, 1024), F32),...]
where the time goes in v5:
time: 80.3 us; the launch traced here: 80.2 us
  Pallas kernels  79.4 us (99%)
    pallas_call x1, Pallas kernels, on_device(): pl.pallas_call(kernel, out_shape=jax.ShapeDtypeStruct((128, 1024), F32),...  79.4 us

profile of v5, /device:TPU:0, one launch (start us, length us, event | category | flops | bytes accessed | tf_op | source)
XLA Modules:
  0.0 80.2 jit_solution(5613176034125622399)
XLA Ops:
  0.0 79.4 %collision.1 = f32[128,1024]{1,0:T(8,128)S(1)} custom-call(f32[2048,1024]{1,0:T(8,128)} %sigma_ret.1, f32[2048,1024]{1,0:T(8,128)} %sigma_less.1, f32[1024,128]{1,0:T(8,128)} %green_less.1, f32[8,16384]{1,0:T(8,128)} %green_ret.1), custom_call_target="tpu_custom_call" | custom-call | tf_op jit(solution)/shard_map/collision/pallas_call | solution.py:421
  79.4 0.8 copy.6

commit v6 on v5

--- a/solution.py
+++ b/solution.py
@@ -37,6 +37,17 @@
 
     y_up, y_down, x_pair = at_col(0, 1), at_col(0, NY - 1), at_col(1, 0)
 
+    def tell(semaphore, peers):
+        for peer in peers:
+            pl.semaphore_signal(semaphore, inc=1, device_id=peer, device_id_type=MESH)
+
+    z_mates = [at_row(0, d, 0) for d in range(1, NZ)]
+    near_row = [(1, 0, 0), (1, 0, 1)] + [(0, d, c) for d in (2, 1, 3) for c in (0, 1)] + [(0, 0, 1)]
+    far_row = [(1, d, c) for d in (2, 1, 3) for c in (0, 1)]
+    near = [y_up, y_down, x_pair] + [at_row(*place) for place in near_row]
+    barrier = pltpu.get_barrier_semaphore()
+    tell(barrier, near)
+
     load_lesser = pltpu.make_async_copy(green_less, lesser.at[0], load_sem.at[0])
     load_mirror = pltpu.make_async_copy(green_ret, mirror, load_sem.at[1])
     load_lesser.start()
@@ -56,16 +67,6 @@
     for t in range(AHEAD):
         stage_copy(0, sigma_ret, t).start()
 
-    def tell(semaphore, peers):
-        for peer in peers:
-            pl.semaphore_signal(semaphore, inc=1, device_id=peer, device_id_type=MESH)
-
-    z_mates = [at_row(0, d, 0) for d in range(1, NZ)]
-    near_row = [(1, 0, 0), (1, 0, 1)] + [(0, d, c) for d in (2, 1, 3) for c in (0, 1)] + [(0, 0, 1)]
-    far_row = [(1, d, c) for d in (2, 1, 3) for c in (0, 1)]
-    near = [y_up, y_down, x_pair] + [at_row(*place) for place in near_row]
-    barrier = pltpu.get_barrier_semaphore()
-    tell(barrier, near)
     pl.semaphore_wait(barrier, len(near))
     tell(ready_sem, z_mates)
 

time: 80.3 us -> 80.5 us (level)
  no operation moved by 1% of the time
where the time goes in v6:
time: 80.5 us; the launch traced here: 80.3 us
  Pallas kernels  79.5 us (99%)
    pallas_call x1, Pallas kernels, on_device(): pl.pallas_call(kernel, out_shape=jax.ShapeDtypeStruct((128, 1024), F32),...  79.5 us

profile of v6, /device:TPU:0, one launch (start us, length us, event | category | flops | bytes accessed | tf_op | source)
XLA Modules:
  0.0 80.3 jit_solution(457746637447406744)
XLA Ops:
  0.0 79.5 %collision.1 = f32[128,1024]{1,0:T(8,128)S(1)} custom-call(f32[2048,1024]{1,0:T(8,128)} %sigma_ret.1, f32[2048,1024]{1,0:T(8,128)} %sigma_less.1, f32[1024,128]{1,0:T(8,128)} %green_less.1, f32[8,16384]{1,0:T(8,128)} %green_ret.1), custom_call_target="tpu_custom_call" | custom-call | tf_op jit(solution)/shard_map/collision/pallas_call | solution.py:422
  79.6 0.8 copy.6
